TPU v7x, 32 devices: a whole 2x2x4 slice. The times are simulated.
32 devices in a mesh: dp: 8 (over y, x, core), sp: 4 (over z).
Axes of the slice: x: 2, y: 2, z: 4, core: 2. Of those that a mesh axis runs over, the one named last changes fastest.
Arguments:
- hidden_in: bfloat16 [32, 1024, 768], P('dp', 'sp'), may hold values from -6 to 6
- time_embed: bfloat16 [32, 128], P('dp'), may hold values from -6 to 6
- ada_weight: bfloat16 [128, 4608], replicated, may hold values from -0.25 to 0.25
- ada_bias: bfloat16 [4608], replicated, may hold values from -1.5 to 1.5
- attn_gain: bfloat16 [768], replicated, may hold values from 0.25 to 1.75
- query_key_value_matrix: bfloat16 [768, 2304], replicated, may hold values from -0.21875 to 0.21875
- attention_output_matrix: bfloat16 [768, 768], replicated, may hold values from -1.75 to 1.75
- mlp_gain: bfloat16 [768], replicated, may hold values from 0.25 to 1.75
- up_projection_matrix: bfloat16 [768, 3072], replicated, may hold values from -0.21875 to 0.21875
- up_bias: bfloat16 [3072], replicated, may hold values from -3 to 3
- down_projection_matrix: bfloat16 [3072, 768], replicated, may hold values from -0.109375 to 0.109375
- down_bias: bfloat16 [768], replicated, may hold values from -3 to 3
- out_cotangent: bfloat16 [32, 1024, 768], P('dp', 'sp'), may hold values from -6 to 6
Outputs:
- output: bfloat16 [32, 1024, 768], P('dp', 'sp')
- hidden_grad: float32 [32, 1024, 768], P('dp', 'sp')
- time_grad: float32 [32, 128], P('dp')
- ada_weight_grad: float32 [128, 4608], P('sp')
- ada_bias_grad: float32 [4608], P('sp')
- attn_gain_grad: float32 [768], P('sp')
- qkv_weight_grad: float32 [768, 2304], P('sp')
- proj_weight_grad: float32 [768, 768], P('sp')
- mlp_gain_grad: float32 [768], P('sp')
- up_weight_grad: float32 [768, 3072], P('sp')
- up_bias_grad: float32 [3072], P('sp')
- down_weight_grad: float32 [3072, 768], P('sp')
- down_bias_grad: float32 [768], P('sp')
All inputs are finite; a program needn't handle non-finite values.
Results may differ from a plain program's by a relative error of at most 0.012.
The roundings to bfloat16 on the way count: a program that leaves them out, or rounds other values in their place, can miss the bound.
Values may be sent and summed in bfloat16 or wider, within the bound.
No kernel may reach another device: no remote copies, remote signals or barrier semaphores. Data moves between devices by JAX's collectives and lax.ppermute only.
A program may use at most 192 MiB of HBM per device.

v0:
```python
import jax
import jax.numpy as jnp
from jax import lax
from jax.sharding import PartitionSpec as P

HEAD_DIM = 64
highest = lax.Precision.HIGHEST
epsilon = 1e-05


def rope_tables(length, columns):
    half_width = columns // 2
    frequency = 10000.0 ** (-(jnp.arange(half_width, dtype=jnp.float32) * 2.0 / columns))
    angles = jnp.arange(length, dtype=jnp.float32)[:, None] * frequency[None, :]
    cos_table = jnp.cos(angles)
    sin_table = jnp.sin(angles)
    cos_table = jnp.concatenate([cos_table, cos_table], axis=-1)[:, None, :]
    sin_table = jnp.concatenate([sin_table, sin_table], axis=-1)[:, None, :]
    return (cos_table, sin_table)


def rotary(values, cos_table, sin_table):
    half_width = values.shape[-1] // 2
    turned = jnp.concatenate([-values[..., half_width:], values[..., :half_width]], axis=-1)
    return values * cos_table + turned * sin_table


def unrotary(gradients, cos_table, sin_table):
    half_width = gradients.shape[-1] // 2
    scaled = gradients * sin_table
    turned = jnp.concatenate([scaled[..., half_width:], -scaled[..., :half_width]], axis=-1)
    return gradients * cos_table + turned


def gelu_tanh(values):
    return jax.nn.gelu(values, approximate=True)


def norm_forward(values):
    center = values - jnp.mean(values, axis=-1, keepdims=True)
    inverse = lax.rsqrt(jnp.mean(center * center, axis=-1, keepdims=True) + epsilon)
    return (center * inverse, inverse)


def norm_backward(grad_normed, normed, inverse):
    first = jnp.mean(grad_normed, axis=-1, keepdims=True)
    second = jnp.mean(grad_normed * normed, axis=-1, keepdims=True)
    return inverse * (grad_normed - first - normed * second)


def rotate_single(single, cos_table, sin_table):
    length = single.shape[0]
    heads_here = single.shape[2] // HEAD_DIM
    shaped = single.astype(jnp.float32).reshape(length, 3, heads_here, HEAD_DIM)
    queries = rotary(shaped[:, 0], cos_table, sin_table).astype(jnp.bfloat16).reshape(length, -1)
    rotated_keys = (
        rotary(shaped[:, 1], cos_table, sin_table).astype(jnp.bfloat16).reshape(length, -1)
    )
    return jnp.stack([queries, rotated_keys, single[:, 2]], axis=1)


def attend_single(rotated):
    length = rotated.shape[0]
    heads_here = rotated.shape[2] // HEAD_DIM
    queries = rotated[:, 0].reshape(length, heads_here, HEAD_DIM)
    rotated_keys = rotated[:, 1].reshape(length, heads_here, HEAD_DIM)
    values = rotated[:, 2].reshape(length, heads_here, HEAD_DIM)
    scores = jnp.einsum(
        "qhd,khd->hqk", queries, rotated_keys, preferred_element_type=jnp.float32
    ) * HEAD_DIM ** (-0.5)
    probabilities = jax.nn.softmax(scores, axis=-1).astype(jnp.bfloat16)
    mixed_heads = jnp.einsum(
        "hqk,khd->qhd", probabilities, values, preferred_element_type=jnp.float32
    )
    return mixed_heads.reshape(length, -1).astype(jnp.bfloat16)


def attend_items(several):
    cos_table, sin_table = rope_tables(several.shape[1], HEAD_DIM)

    def one_single(single):
        rotated = rotate_single(single, cos_table, sin_table)
        return (attend_single(rotated), rotated)

    return lax.map(one_single, several)


def backward_single(rotated, grad_mixed, cos_table, sin_table):
    length = rotated.shape[0]
    heads_here = rotated.shape[2] // HEAD_DIM
    queries = rotated[:, 0].reshape(length, heads_here, HEAD_DIM)
    rotated_keys = rotated[:, 1].reshape(length, heads_here, HEAD_DIM)
    values = rotated[:, 2].reshape(length, heads_here, HEAD_DIM)
    grad_heads = grad_mixed.reshape(length, heads_here, HEAD_DIM)
    scale_factor = HEAD_DIM ** (-0.5)
    scores = (
        jnp.einsum("qhd,khd->hqk", queries, rotated_keys, preferred_element_type=jnp.float32)
        * scale_factor
    )
    probabilities = jax.nn.softmax(scores, axis=-1)
    probs_low = probabilities.astype(jnp.bfloat16)
    grad_values = jnp.einsum(
        "hqk,qhd->khd", probs_low, grad_heads, preferred_element_type=jnp.float32
    )
    grad_probs = jnp.einsum("qhd,khd->hqk", grad_heads, values, preferred_element_type=jnp.float32)
    row_terms = jnp.sum(probabilities * grad_probs, axis=-1, keepdims=True)
    grad_scores = (probabilities * (grad_probs - row_terms)).astype(jnp.bfloat16)
    grad_queries = (
        jnp.einsum("hqk,khd->qhd", grad_scores, rotated_keys, preferred_element_type=jnp.float32)
        * scale_factor
    )
    grad_keys = (
        jnp.einsum("hqk,qhd->khd", grad_scores, queries, preferred_element_type=jnp.float32)
        * scale_factor
    )
    grad_queries = unrotary(grad_queries, cos_table, sin_table)
    grad_keys = unrotary(grad_keys, cos_table, sin_table)
    stacked = jnp.stack(
        [
            grad_queries.reshape(length, -1),
            grad_keys.reshape(length, -1),
            grad_values.reshape(length, -1),
        ],
        axis=1,
    )
    return stacked.astype(jnp.bfloat16)


def body(
    hidden_in,
    time_embed,
    ada_weight,
    ada_bias,
    attn_gain,
    query_key_value_matrix,
    attention_output_matrix,
    mlp_gain,
    up_projection_matrix,
    up_bias,
    down_projection_matrix,
    down_bias,
    out_cotangent,
):
    seq_count, local_len, width = hidden_in.shape
    residual = hidden_in.astype(jnp.float32)
    ada_full = ada_weight.astype(jnp.float32)
    timing = time_embed.astype(jnp.float32)
    modulation = jnp.dot(timing, ada_full, precision=highest) + ada_bias.astype(jnp.float32)
    shift_attn, scale_attn, gate_attn, shift_mlp, scale_mlp, gate_mlp = jnp.split(
        modulation[:, None, :], 6, axis=-1
    )
    gain_attn = attn_gain.astype(jnp.float32)
    gain_mlp = mlp_gain.astype(jnp.float32)
    normed_attn, inverse_attn = norm_forward(residual)
    attention_modulated_input = (normed_attn * gain_attn * (1.0 + scale_attn) + shift_attn).astype(
        jnp.bfloat16
    )
    qkv_seq = jnp.einsum(
        "tig,gn->tin",
        attention_modulated_input,
        query_key_value_matrix,
        preferred_element_type=jnp.float32,
    )
    qkv_seq = qkv_seq.astype(jnp.bfloat16).reshape(seq_count, local_len, 3, width)
    mixed_heads, kept_heads = attend_items(
        lax.all_to_all(qkv_seq, "sp", split_axis=3, concat_axis=1, tiled=True)
    )
    attention_mixed_sequence = lax.all_to_all(
        mixed_heads, "sp", split_axis=1, concat_axis=2, tiled=True
    )
    projected = jnp.einsum(
        "tig,gn->tin",
        attention_mixed_sequence,
        attention_output_matrix,
        preferred_element_type=jnp.float32,
    )
    middle = residual + gate_attn * projected
    normed_mlp, inverse_mlp = norm_forward(middle)
    feedforward_modulated_input = (normed_mlp * gain_mlp * (1.0 + scale_mlp) + shift_mlp).astype(
        jnp.bfloat16
    )
    pre_act = jnp.einsum(
        "xac,cz->xaz",
        feedforward_modulated_input,
        up_projection_matrix,
        preferred_element_type=jnp.float32,
    ) + up_bias.astype(jnp.float32)
    activated_f, gelu_pullback = jax.vjp(gelu_tanh, pre_act)
    gelu_activation = activated_f.astype(jnp.bfloat16)
    down_out = jnp.einsum(
        "ngw,wo->ngo", gelu_activation, down_projection_matrix, preferred_element_type=jnp.float32
    ) + down_bias.astype(jnp.float32)
    output = (middle + gate_mlp * down_out).astype(jnp.bfloat16)
    grad_out = out_cotangent.astype(jnp.float32)
    grad_gate_mlp = jnp.sum(grad_out * down_out, axis=1)
    down_output_gradient = (gate_mlp * grad_out).astype(jnp.bfloat16)
    grad_down_bias = jnp.sum(down_output_gradient.astype(jnp.float32), axis=(0, 1))
    grad_down_weight = jnp.einsum(
        "qpj,qpi->ji", gelu_activation, down_output_gradient, preferred_element_type=jnp.float32
    )
    activation_gradient = jnp.einsum(
        "eoa,ta->eot",
        down_output_gradient,
        down_projection_matrix,
        preferred_element_type=jnp.float32,
    )
    preactivation_gradient = gelu_pullback(activation_gradient)[0].astype(jnp.bfloat16)
    grad_up_bias = jnp.sum(preactivation_gradient.astype(jnp.float32), axis=(0, 1))
    grad_up_weight = jnp.einsum(
        "rqm,rqc->mc",
        feedforward_modulated_input,
        preactivation_gradient,
        preferred_element_type=jnp.float32,
    )
    grad_mod_mlp = jnp.einsum(
        "qbz,nz->qbn",
        preactivation_gradient,
        up_projection_matrix,
        preferred_element_type=jnp.float32,
    )
    grad_shift_mlp = jnp.sum(grad_mod_mlp, axis=1)
    grad_scale_mlp = jnp.sum(grad_mod_mlp * normed_mlp * gain_mlp, axis=1)
    grad_mlp_gain = jnp.sum(grad_mod_mlp * (1.0 + scale_mlp) * normed_mlp, axis=(0, 1))
    grad_middle = grad_out + norm_backward(
        grad_mod_mlp * gain_mlp * (1.0 + scale_mlp), normed_mlp, inverse_mlp
    )
    grad_gate_attn = jnp.sum(grad_middle * projected, axis=1)
    projection_output_gradient = (gate_attn * grad_middle).astype(jnp.bfloat16)
    grad_proj_weight = jnp.einsum(
        "kuv,kuf->vf",
        attention_mixed_sequence,
        projection_output_gradient,
        preferred_element_type=jnp.float32,
    )
    grad_mixed = jnp.einsum(
        "oam,ym->oay",
        projection_output_gradient,
        attention_output_matrix,
        preferred_element_type=jnp.float32,
    ).astype(jnp.bfloat16)
    grad_heads = lax.all_to_all(grad_mixed, "sp", split_axis=2, concat_axis=1, tiled=True)
    cos_table, sin_table = rope_tables(grad_heads.shape[1], HEAD_DIM)

    def kept_pair(pair):
        return backward_single(pair[0], pair[1], cos_table, sin_table)

    grad_qkv_heads = lax.map(kept_pair, (kept_heads, grad_heads))
    query_key_value_gradient = lax.all_to_all(
        grad_qkv_heads, "sp", split_axis=1, concat_axis=3, tiled=True
    ).reshape(seq_count, local_len, 3 * width)
    grad_qkv_weight = jnp.einsum(
        "kuv,kuf->vf",
        attention_modulated_input,
        query_key_value_gradient,
        preferred_element_type=jnp.float32,
    )
    grad_mod_attn = jnp.einsum(
        "oam,ym->oay",
        query_key_value_gradient,
        query_key_value_matrix,
        preferred_element_type=jnp.float32,
    )
    grad_shift_attn = jnp.sum(grad_mod_attn, axis=1)
    grad_scale_attn = jnp.sum(grad_mod_attn * normed_attn * gain_attn, axis=1)
    grad_attn_gain = jnp.sum(grad_mod_attn * (1.0 + scale_attn) * normed_attn, axis=(0, 1))
    hidden_grad = grad_middle + norm_backward(
        grad_mod_attn * gain_attn * (1.0 + scale_attn), normed_attn, inverse_attn
    )
    grad_modulation = jnp.concatenate(
        [
            grad_shift_attn,
            grad_scale_attn,
            grad_gate_attn,
            grad_shift_mlp,
            grad_scale_mlp,
            grad_gate_mlp,
        ],
        axis=-1,
    )
    full_modulation = lax.psum(grad_modulation.astype(jnp.bfloat16), "sp").astype(jnp.float32)
    time_grad = jnp.dot(full_modulation, ada_full.T, precision=highest)
    grad_ada_weight = jnp.dot(timing.T, grad_modulation, precision=highest)
    grad_ada_bias = jnp.sum(grad_modulation, axis=0)
    shards = (
        lax.psum_scatter(grad_ada_weight, "sp", scatter_dimension=0, tiled=True),
        lax.psum_scatter(grad_ada_bias, "sp", scatter_dimension=0, tiled=True),
        lax.psum_scatter(grad_attn_gain, "sp", scatter_dimension=0, tiled=True),
        lax.psum_scatter(grad_qkv_weight, "sp", scatter_dimension=0, tiled=True),
        lax.psum_scatter(grad_proj_weight, "sp", scatter_dimension=0, tiled=True),
        lax.psum_scatter(grad_mlp_gain, "sp", scatter_dimension=0, tiled=True),
        lax.psum_scatter(grad_up_weight, "sp", scatter_dimension=0, tiled=True),
        lax.psum_scatter(grad_up_bias, "sp", scatter_dimension=0, tiled=True),
        lax.psum_scatter(grad_down_weight, "sp", scatter_dimension=0, tiled=True),
        lax.psum_scatter(grad_down_bias, "sp", scatter_dimension=0, tiled=True),
    )
    summed = lax.psum(
        (
            shards[0],
            shards[1],
            shards[2],
            shards[3],
            shards[4],
            shards[5],
            shards[6],
            shards[7],
            shards[8],
            shards[9],
        ),
        "dp",
    )
    return (
        output,
        hidden_grad,
        time_grad,
        summed[0],
        summed[1],
        summed[2],
        summed[3],
        summed[4],
        summed[5],
        summed[6],
        summed[7],
        summed[8],
        summed[9],
    )


def solution(mesh):
    return jax.shard_map(
        body,
        mesh=mesh,
        in_specs=(
            P("dp", "sp", None),
            P("dp", None),
            P(),
            P(),
            P(),
            P(),
            P(),
            P(),
            P(),
            P(),
            P(),
            P(),
            P("dp", "sp", None),
        ),
        out_specs=(
            P("dp", "sp", None),
            P("dp", "sp", None),
            P("dp", None),
            P("sp", None),
            P("sp"),
            P("sp"),
            P("sp", None),
            P("sp", None),
            P("sp"),
            P("sp", None),
            P("sp"),
            P("sp", None),
            P("sp"),
        ),
        check_vma=False,
    )
```

profile of v0, /device:TPU:0, one launch (start us, length us, event | category | flops | bytes accessed | tf_op | source)
XLA Modules:
  0.0 1487.4 jit_solution(7449121573997723435)
XLA Ops:
  42.4 103.3 %all-to-all-done = bf16[4,256,3,768]{1,0,2,3:T(4,128)(2,1)} async-done(((bf16[4,256,3,768]{1,0,2,3:T(4,128)(2,1)}), bf16[4,256,3,768]{1,0,2,3:T(4,128)(2,1)}, u32[]{:S(2)}, u32[]{:S(2)}) %all-to-all-start) | async-done | bytes 4718624 | tf_op jit(solution)/shard_map/all_to_all | solution.py:166
  154.2 99.2 %while.22 = (s32[]{:T(128)}, bf16[4,1024,192]{1,2,0:T(8,128)(2,1)}, bf16[4,1024,3,192]{1,3,2,0:T(8,128)(2,1)}, bf16[4,1024,3,192]{1,3,2,0:T(8,128)(2,1)}, f32[10...) while((s32[]{:T(128)}, bf16[4,1024,192]{1,2,0:T(8,128)(2,1)}, ...), condition=%wide.region_5.6_spmd, body=%wide.region_2.5_spmd.sunk | while | flops 828703744 | bytes 63856824 | solution.py:85
  187.5 9.6 fusion.151
  265.7 44.1 %all-to-all-done.1 = bf16[4,1024,192]{2,0,1:T(4,128)(2,1)} async-done(((bf16[4,1024,192]{2,0,1:T(4,128)(2,1)}), bf16[4,1024,192]{2,0,1:T(4,128)(2,1)}, u32[]{:S(2)}, u32[]{:S(2)}) %all-to-all-start.1) | async-done | bytes 1572896 | tf_op jit(solution)/shard_map/all_to_all | solution.py:168
  327.0 15.7 %convert_reduce_fusion = (f32[3072]{0:T(1024)}, bf16[4,256,3072]{2,1,0:T(8,128)(2,1)S(1)}) fusion(f32[4,256,3072]{2,1,0:T(8,128)} %fusion.44, f32[3072]{0:T(1024)S(1)} %copy-done.40, bf16[3072,768]{1,0:T(8,128)(2,1)} %param.27, bf16[4,256,768]{2,1,0:T(8,128)(2,1)S(1)} %copy-done.49, f32[4,768]{1,0:T(4,128)S(1)} %copy-done.38), kind=kOutput, calls=%fused_computation.65 | convolution fusion | flops 4906546176 | bytes 25202688 | tf_op jit(solution)/shard_map/eoa,ta->eot/dot_general | solution.py:201
  342.8 13.0 multiply_reduce_fusion.3
  355.8 15.4 %convert_reduce_fusion.2 = (f32[768]{0:T(1024)}, f32[4,768]{1,0:T(4,128)}, bf16[4,256,768]{2,1,0:T(8,128)(2,1)}, f32[4,768]{1,0:T(4,128)}, f32[4,256,768]{2,1,0:T(8,128)S(1)}) fusion(bf16[4,256,768]{2,1,0:T(8,128)(2,1)S(1)} %copy-done.49, f32[4,768]{1,0:T(4,128)S(1)} %copy-done.38, f32[768]{0:T(1024)S(1)} %copy-done.46, ...), kind=kOutput, calls=%fused_computation.111 | convolution fusion | flops 4880589824 | bytes 33117184 | tf_op jit(solution)/shard_map/ngw,wo->ngo/dot_general | solution.py:190
  379.2 40.1 %all_to_all.69 = bf16[4,256,768]{1,0,2:T(4,128)(2,1)S(1)} all-to-all(bf16[4,256,768]{1,0,2:T(4,128)(2,1)} %copy.129), channel_id=1, replica_groups=mesh['dp'=8,'sp'=4] {'sp'}, dimensions={2} | all-to-all | bytes 3145728 | tf_op jit(solution)/shard_map/all_to_all | solution.py:241
  423.7 168.4 %while.23 = (s32[]{:T(128)}, bf16[4,1024,3,192]{1,3,2,0:T(8,128)(2,1)}, bf16[4,1024,3,192]{1,3,2,0:T(8,128)(2,1)}, bf16[4,1024,192]{1,2,0:T(8,128)(2,1)}, f32[10...) while((s32[]{:T(128)}, bf16[4,1024,3,192]{1,3,2,0:T(8,128)(2,1)}, ...), condition=%wide.region_14.15_spmd, body=%wide.region_10.0_spmd.sunk | while | flops 2057041920 | bytes 176759088 | solution.py:247
  592.1 10.3 copy.132
  602.4 144.0 %all_to_all.70 = bf16[4,1024,3,192]{3,0,2,1:T(4,128)(2,1)} all-to-all(bf16[4,1024,3,192]{3,0,2,1:T(4,128)(2,1)} %copy.132), channel_id=1, replica_groups=mesh['dp'=8,'sp'=4] {'sp'}, dimensions={1} | all-to-all | bytes 9437184 | tf_op jit(solution)/shard_map/all_to_all | solution.py:248
  746.5 10.3 copy.134
  756.8 9.9 fusion.67
  779.2 10.9 convolution_bitcast_fusion.4
  790.8 14.0 convolution_bitcast_fusion.3
  805.5 10.2 convolution_bitcast_fusion.5
  824.4 46.7 %reduce-scatter.10.cloned.1.call-done = f32[192,768]{1,0:T(8,128)} async-done(((f32[768,768]{1,0:T(8,128)}), f32[192,768]{1,0:T(8,128)}) %reduce-scatter.10.cloned.1.call-update) | async-done | bytes 589840 | tf_op jit(solution)/shard_map/reduce_scatter | solution.py:289
  871.2 163.2 %reduce-scatter.12.cloned.1.call-done = f32[192,3072]{1,0:T(8,128)} async-done(((f32[768,3072]{1,0:T(8,128)}), f32[192,3072]{1,0:T(8,128)}) %reduce-scatter.12.cloned.1.call-update) | async-done | bytes 2359312 | tf_op jit(solution)/shard_map/reduce_scatter | solution.py:291
  1034.3 164.4 %reduce-scatter.14.cloned.1.call-done = f32[768,768]{1,0:T(8,128)} async-done(((f32[3072,768]{1,0:T(8,128)}), f32[768,768]{1,0:T(8,128)}) %reduce-scatter.14.cloned.1.call-update) | async-done | bytes 2359312 | tf_op jit(solution)/shard_map/reduce_scatter | solution.py:293
  1198.7 126.5 %reduce-scatter.8.cloned.1.call-done = f32[192,2304]{1,0:T(8,128)} async-done(((f32[768,2304]{1,0:T(8,128)}), f32[192,2304]{1,0:T(8,128)}) %reduce-scatter.8.cloned.1.call-update) | async-done | bytes 1769488 | tf_op jit(solution)/shard_map/reduce_scatter | solution.py:288
  1330.6 19.7 %all-reduce.7 = (f32[4608]{0:T(1024)}, f32[768]{0:T(1024)}, f32[768]{0:T(1024)}, f32[3072]{0:T(1024)}, f32[768]{0:T(1024)}) all-reduce(f32[4608]{0:T(1024)} %get-tuple-element.255, f32[768]{0:T(1024)} %get-tuple-element.162, f32[768]{0:T(1024)} %get-tuple-element.159, ...), channel_id=3, replica_groups=mesh['dp'=8,'sp'=4] {'sp'}, use_global_device_ids=true, to_apply=%region_27.28.clone | all-reduce | flops 9984 | bytes 79872
  1357.1 24.7 %all-reduce.5 = (f32[1152]{0:T(1024)}, f32[192]{0:T(256)}, f32[192]{0:T(256)}, f32[768]{0:T(1024)}, f32[192]{0:T(256)}) all-reduce(f32[1152]{0:T(1024)} %dynamic-slice.1, f32[192]{0:T(256)} %dynamic-slice.3, f32[192]{0:T(256)} %dynamic-slice.5, f32[768]{0:T(1024)} %dynamic-slice.7, ...), channel_id=1, replica_groups=mesh['dp'=8,'sp'=4] {'dp'}, use_global_device_ids=true, to_apply=%region_28.29 | all-reduce | flops 2496 | bytes 19968 | tf_op jit(solution)/shard_map/psum | solution.py:296
  1381.8 17.2 %psum.77 = bf16[4,4608]{1,0:T(4,128)(2,1)} all-reduce(bf16[4,4608]{1,0:T(4,128)(2,1)} %get-tuple-element.256), channel_id=1, replica_groups=mesh['dp'=8,'sp'=4] {'sp'}, use_global_device_ids=true, to_apply=%region_23.24 | all-reduce | flops 18432 | bytes 73728 | tf_op jit(solution)/shard_map/psum | solution.py:280
  1407.9 62.5 %all-reduce.10.cloned.1.call-done = (f32[32,4608]{0,1:T(8,128)}, f32[192,2304]{1,0:T(8,128)}, f32[192,768]{1,0:T(8,128)}, f32[192,3072]{1,0:T(8,128)}, f32[768,768]{1,0:T(8,128)}) async-done(((f32[32,4608]{0,1:T(8,128)}, f32[192,2304]{1,0:T(8,128)}, f32[192,768]{1,0:T(8,128)}, f32[192,3072]{1,0:T(8,128)}, f32[768,768]{1,0:T(8,128)}), (f32[32,4608]{0,1:T(8,128)}, f32[192,2304]{1,0:T(8,128)}, ...) | async-done | bytes 7667728 | tf_op jit(solution)/shard_map/psum | solution.py:296
  (352 shorter events, 393.8 us)
Async XLA Ops:
  34.5 111.3 %all-to-all-start = ((bf16[4,256,3,768]{1,0,2,3:T(4,128)(2,1)}), bf16[4,256,3,768]{1,0,2,3:T(4,128)(2,1)}, u32[]{:S(2)}, u32[]{:S(2)}) async-start(bf16[4,256,3,768]{1,0,2,3:T(4,128)(2,1)} %copy.122), calls=%async_computation | async-start | bytes 9437184 | tf_op jit(solution)/shard_map/all_to_all | solution.py:166
  257.5 56.4 %copy-start.31 = (f32[4,768]{1,0:T(4,128)S(1)}, f32[4,768]{1,0:T(4,128)}, u32[]{:S(2)}) copy-start(f32[4,768]{1,0:T(4,128)} %get-tuple-element.262) | copy-start | bytes 36868
  257.5 52.3 %all-to-all-start.1 = ((bf16[4,1024,192]{2,0,1:T(4,128)(2,1)}), bf16[4,1024,192]{2,0,1:T(4,128)(2,1)}, u32[]{:S(2)}, u32[]{:S(2)}) async-start(bf16[4,1024,192]{2,0,1:T(4,128)(2,1)} %copy.125), calls=%async_computation.1 | async-start | bytes 4194304 | tf_op jit(solution)/shard_map/all_to_all | solution.py:168
  262.1 559.2 %reduce-scatter.16.cloned.1.call-start = ((), (), s32[]{:S(2)}) async-start(), calls=%async_computation.13 | async-start | bytes 2949120
  263.1 92.7 %copy-start.24 = (f32[768]{0:T(1024)}, f32[768]{0:T(1024)S(1)}, u32[]{:S(2)}) copy-start(f32[768]{0:T(1024)S(1)} %convert_element_type.129) | copy-start | bytes 9220
  318.0 37.7 %copy-start.8 = (f32[4,256,768]{2,1,0:T(8,128)}, f32[4,256,768]{2,1,0:T(8,128)S(1)}, u32[]{:S(2)}) copy-start(f32[4,256,768]{2,1,0:T(8,128)S(1)} %get-tuple-element.217) | copy-start | bytes 9437188
  318.1 37.7 %copy-start.26 = (f32[4,256]{1,0:T(4,128)}, f32[4,256]{1,0:T(4,128)S(1)}, u32[]{:S(2)}) copy-start(f32[4,256]{1,0:T(4,128)S(1)} %broadcast_multiply_fusion.6) | copy-start | bytes 12292
  318.6 37.2 %copy-start.27 = (f32[4,256]{1,0:T(4,128)}, f32[4,256]{1,0:T(4,128)S(1)}, u32[]{:S(2)}) copy-start(f32[4,256]{1,0:T(4,128)S(1)} %add_rsqrt_fusion) | copy-start | bytes 12292
  342.8 13.0 copy-start.13
  342.8 13.0 copy-start.46
  355.8 17.1 %copy-start.18 = (bf16[768,768]{1,0:T(8,128)(2,1)S(1)}, bf16[768,768]{1,0:T(8,128)(2,1)}, u32[]{:S(2)}) copy-start(bf16[768,768]{1,0:T(8,128)(2,1)} %param.23) | copy-start | bytes 3538948
  439.3 8.4 copy-start.12
  746.5 10.3 copy-start.29
  746.5 10.3 copy-start.33
  756.7 10.0 copy-start.44
  756.7 10.0 copy-start.42
  756.7 10.0 copy-start.41
  756.8 10.0 copy-start.43
  756.8 10.6 copy-start.48
  773.9 97.2 %reduce-scatter.10.cloned.1.call-start = ((), (), s32[]{:S(2)}) async-start(), calls=%async_computation.10 | async-start | bytes 2949120 | tf_op jit(solution)/shard_map/reduce_scatter | solution.py:289
  779.1 255.2 %reduce-scatter.12.cloned.1.call-start = ((), (), s32[]{:S(2)}) async-start(), calls=%async_computation.11 | async-start | bytes 11796480 | tf_op jit(solution)/shard_map/reduce_scatter | solution.py:291
  790.1 408.6 %reduce-scatter.14.cloned.1.call-start = ((), (), s32[]{:S(2)}) async-start(), calls=%async_computation.12 | async-start | bytes 11796480 | tf_op jit(solution)/shard_map/reduce_scatter | solution.py:293
  804.8 520.4 %reduce-scatter.8.cloned.1.call-start = ((), (), s32[]{:S(2)}) async-start(), calls=%async_computation.9 | async-start | bytes 8847360 | tf_op jit(solution)/shard_map/reduce_scatter | solution.py:288
  815.7 654.7 %all-reduce.10.cloned.1.call-start = ((), (), s32[]{:S(2)}) async-start(), calls=%async_computation.14 | async-start | bytes 18874368 | tf_op jit(solution)/shard_map/psum | solution.py:296
  (66 other events, 264.4 us)
Sparse Core Ops, SparseCore 0:
  774.0 47.2 reduce-scatter.15
  823.6 47.5 reduce-scatter.9
  873.5 160.7 reduce-scatter.11
  1036.5 162.1 reduce-scatter.13
  1200.8 124.3 reduce-scatter.7
  1329.9 140.4 all-reduce.9
where the time goes:
time: 1500 us; the launch traced here: 1490 us
  waiting for transfers between devices  716 us (48%)
  matrix products  284 us (19%)
  blocking collectives  246 us (16%)
  local copies, waits for them, and re-layouts  137 us (9%)
  other arithmetic  74.4 us (5%)
  between operations  16.9 us (1%)
    reduce_scatter x1, waiting for transfers between devices, body(): lax.psum_scatter(grad_down_weight, 'sp', scatter_dimension=0, tiled=True)  164 us
    reduce_scatter x1, waiting for transfers between devices, body(): lax.psum_scatter(grad_up_weight, 'sp', scatter_dimension=0, tiled=True)  163 us
    all_to_all x1, blocking collectives, body(): lax.all_to_all(grad_qkv_heads, 'sp', split_axis=1, concat_axis=3, tiled=T...  144 us
    reduce_scatter x1, waiting for transfers between devices, body(): lax.psum_scatter(grad_qkv_weight, 'sp', scatter_dimension=0, tiled=True)  127 us
    all_to_all x1, waiting for transfers between devices, body(): lax.all_to_all(qkv_seq, 'sp', split_axis=3, concat_axis=1, tiled=True)  103 us
    psum x1, waiting for transfers between devices, body(): lax.psum((shards[0], shards[1], shards[2], shards[3], shards[4], shards[5...  62.5 us
    reduce_scatter x1, waiting for transfers between devices, body(): lax.psum_scatter(grad_proj_weight, 'sp', scatter_dimension=0, tiled=True)  46.7 us
    all_to_all x1, waiting for transfers between devices, body(): lax.all_to_all(mixed_heads, 'sp', split_axis=1, concat_axis=2, tiled=True)  44.1 us
  transfers between devices with their start and end apart: 8, of which 8 were waited for; matrix products, arithmetic and copies ran while one was open for 5% of the time, Pallas kernels for 0%

commit v1 on v0

--- a/solution.py
+++ b/solution.py
@@ -6,6 +6,15 @@
 HEAD_DIM = 64
 highest = lax.Precision.HIGHEST
 epsilon = 1e-05
+move_limits = lambda vec: jnp.concatenate(
+    lax.all_to_all(
+        jnp.stack(jnp.split(vec, lax.axis_size("sp"), axis=1)),
+        axis_name="sp",
+        split_axis=0,
+        concat_axis=0,
+    ),
+    axis=3,
+)
 
 
 def rope_tables(length, columns):
@@ -245,9 +254,7 @@
         return backward_single(pair[0], pair[1], cos_table, sin_table)
 
     grad_qkv_heads = lax.map(kept_pair, (kept_heads, grad_heads))
-    query_key_value_gradient = lax.all_to_all(
-        grad_qkv_heads, "sp", split_axis=1, concat_axis=3, tiled=True
-    ).reshape(seq_count, local_len, 3 * width)
+    query_key_value_gradient = move_limits(grad_qkv_heads).reshape(seq_count, local_len, 3 * width)
     grad_qkv_weight = jnp.einsum(
         "kuv,kuf->vf",
         attention_modulated_input,

time: 1500 us -> 1440 us (0.960)
  blocking collectives: 246 us -> 208 us
  local copies, waits for them, and re-layouts: 137 us -> 121 us
    all_to_all x1, blocking collectives: 144 us -> 107 us  [lax.all_to_all(jnp.stack(jnp.split(vec, lax.axis_size('sp'), axis=1)), ax...]
where the time goes in v1:
time: 1440 us; the launch traced here: 1430 us
  waiting for transfers between devices  716 us (50%)
  matrix products  281 us (20%)
  blocking collectives  208 us (14%)
  local copies, waits for them, and re-layouts  121 us (8%)
  other arithmetic  75.1 us (5%)
  between operations  17 us (1%)
    reduce_scatter x1, waiting for transfers between devices, body(): lax.psum_scatter(grad_down_weight, 'sp', scatter_dimension=0, tiled=True)  164 us
    reduce_scatter x1, waiting for transfers between devices, body(): lax.psum_scatter(grad_up_weight, 'sp', scatter_dimension=0, tiled=True)  163 us
    reduce_scatter x1, waiting for transfers between devices, body(): lax.psum_scatter(grad_qkv_weight, 'sp', scatter_dimension=0, tiled=True)  126 us
    all_to_all x1, blocking collectives, lax.all_to_all(jnp.stack(jnp.split(vec, lax.axis_size('sp'), axis=1)), ax...  107 us
    all_to_all x1, waiting for transfers between devices, body(): lax.all_to_all(qkv_seq, 'sp', split_axis=3, concat_axis=1, tiled=True)  103 us
    psum x1, waiting for transfers between devices, body(): lax.psum((shards[0], shards[1], shards[2], shards[3], shards[4], shards[5...  62.5 us
    reduce_scatter x1, waiting for transfers between devices, body(): lax.psum_scatter(grad_proj_weight, 'sp', scatter_dimension=0, tiled=True)  46.7 us
    all_to_all x1, waiting for transfers between devices, body(): lax.all_to_all(mixed_heads, 'sp', split_axis=1, concat_axis=2, tiled=True)  44.1 us
  transfers between devices with their start and end apart: 8, of which 8 were waited for; matrix products, arithmetic and copies ran while one was open for 5% of the time, Pallas kernels for 0%

profile of v1, /device:TPU:0, one launch (start us, length us, event | category | flops | bytes accessed | tf_op | source)
XLA Modules:
  0.0 1431.8 jit_solution(4447755043486313630)
XLA Ops:
  42.4 103.3 %all-to-all-done = bf16[4,256,3,768]{1,0,2,3:T(4,128)(2,1)} async-done(((bf16[4,256,3,768]{1,0,2,3:T(4,128)(2,1)}), bf16[4,256,3,768]{1,0,2,3:T(4,128)(2,1)}, u32[]{:S(2)}, u32[]{:S(2)}) %all-to-all-start) | async-done | bytes 4718624 | tf_op jit(solution)/shard_map/all_to_all | solution.py:175
  154.3 99.2 %while.22 = (s32[]{:T(128)}, bf16[4,1024,192]{1,2,0:T(8,128)(2,1)}, bf16[4,1024,3,192]{1,3,2,0:T(8,128)(2,1)}, bf16[4,1024,3,192]{1,3,2,0:T(8,128)(2,1)}, f32[10...) while((s32[]{:T(128)}, bf16[4,1024,192]{1,2,0:T(8,128)(2,1)}, ...), condition=%wide.region_5.6_spmd, body=%wide.region_2.5_spmd.sunk | while | flops 828703744 | bytes 63856824 | solution.py:94
  162.8 9.6 fusion.151
  187.6 9.6 fusion.151
  212.4 9.6 fusion.151
  237.2 9.6 fusion.151
  265.8 44.1 %all-to-all-done.1 = bf16[4,1024,192]{2,0,1:T(4,128)(2,1)} async-done(((bf16[4,1024,192]{2,0,1:T(4,128)(2,1)}), bf16[4,1024,192]{2,0,1:T(4,128)(2,1)}, u32[]{:S(2)}, u32[]{:S(2)}) %all-to-all-start.1) | async-done | bytes 1572896 | tf_op jit(solution)/shard_map/all_to_all | solution.py:177
  327.1 15.7 %convert_reduce_fusion = (f32[3072]{0:T(1024)}, bf16[4,256,3072]{2,1,0:T(8,128)(2,1)S(1)}) fusion(f32[4,256,3072]{2,1,0:T(8,128)} %fusion.44, f32[3072]{0:T(1024)S(1)} %copy-done.44, bf16[3072,768]{1,0:T(8,128)(2,1)} %param.27, bf16[4,256,768]{2,1,0:T(8,128)(2,1)S(1)} %copy-done.53, f32[4,768]{1,0:T(4,128)S(1)} %copy-done.42), kind=kOutput, calls=%fused_computation.65 | convolution fusion | flops 4906546176 | bytes 25202688 | tf_op jit(solution)/shard_map/eoa,ta->eot/dot_general | solution.py:210
  342.9 13.0 multiply_reduce_fusion.3
  355.9 15.4 %convert_reduce_fusion.2 = (f32[768]{0:T(1024)}, f32[4,768]{1,0:T(4,128)}, bf16[4,256,768]{2,1,0:T(8,128)(2,1)}, f32[4,768]{1,0:T(4,128)}, f32[4,256,768]{2,1,0:T(8,128)S(1)}) fusion(bf16[4,256,768]{2,1,0:T(8,128)(2,1)S(1)} %copy-done.53, f32[4,768]{1,0:T(4,128)S(1)} %copy-done.42, f32[768]{0:T(1024)S(1)} %copy-done.50, ...), kind=kOutput, calls=%fused_computation.112 | convolution fusion | flops 4880589824 | bytes 33117184 | tf_op jit(solution)/shard_map/ngw,wo->ngo/dot_general | solution.py:199
  379.3 40.1 %all_to_all.59 = bf16[4,256,768]{1,0,2:T(4,128)(2,1)S(1)} all-to-all(bf16[4,256,768]{1,0,2:T(4,128)(2,1)} %copy.124), channel_id=1, replica_groups=mesh['dp'=8,'sp'=4] {'sp'}, dimensions={2} | all-to-all | bytes 3145728 | tf_op jit(solution)/shard_map/all_to_all | solution.py:250
  423.7 168.6 %while.23 = (s32[]{:T(128)}, bf16[4,1024,3,192]{1,3,2,0:T(8,128)(2,1)}, bf16[4,1024,3,192]{1,3,2,0:T(8,128)(2,1)}, bf16[4,1024,192]{1,2,0:T(8,128)(2,1)}, f32[10...) while((s32[]{:T(128)}, bf16[4,1024,3,192]{1,3,2,0:T(8,128)(2,1)}, ...), condition=%wide.region_14.15_spmd, body=%wide.region_10.0_spmd.sunk | while | flops 2057041920 | bytes 176759088 | solution.py:256
  595.9 106.6 %all_to_all.60 = bf16[4,4,256,3,192]{2,4,3,1,0:T(8,128)(2,1)S(1)} all-to-all(bf16[4,4,256,3,192]{2,4,3,1,0:T(8,128)(2,1)S(1)} %pad_maximum_fusion), channel_id=1, replica_groups=mesh['dp'=8,'sp'=4] {'sp'}, dimensions={0} | all-to-all | bytes 9437184 | tf_op jit(solution)/shard_map/all_to_all | solution.py:10
  723.8 10.9 convolution_bitcast_fusion.4
  735.4 13.7 convolution_bitcast_fusion.3
  749.8 10.2 convolution_bitcast_fusion.5
  768.8 46.7 %reduce-scatter.10.cloned.1.call-done = f32[192,768]{1,0:T(8,128)} async-done(((f32[768,768]{1,0:T(8,128)}), f32[192,768]{1,0:T(8,128)}) %reduce-scatter.10.cloned.1.call-update) | async-done | bytes 589840 | tf_op jit(solution)/shard_map/reduce_scatter | solution.py:296
  815.6 163.2 %reduce-scatter.12.cloned.1.call-done = f32[192,3072]{1,0:T(8,128)} async-done(((f32[768,3072]{1,0:T(8,128)}), f32[192,3072]{1,0:T(8,128)}) %reduce-scatter.12.cloned.1.call-update) | async-done | bytes 2359312 | tf_op jit(solution)/shard_map/reduce_scatter | solution.py:298
  978.7 164.4 %reduce-scatter.14.cloned.1.call-done = f32[768,768]{1,0:T(8,128)} async-done(((f32[3072,768]{1,0:T(8,128)}), f32[768,768]{1,0:T(8,128)}) %reduce-scatter.14.cloned.1.call-update) | async-done | bytes 2359312 | tf_op jit(solution)/shard_map/reduce_scatter | solution.py:300
  1143.1 126.5 %reduce-scatter.8.cloned.1.call-done = f32[192,2304]{1,0:T(8,128)} async-done(((f32[768,2304]{1,0:T(8,128)}), f32[192,2304]{1,0:T(8,128)}) %reduce-scatter.8.cloned.1.call-update) | async-done | bytes 1769488 | tf_op jit(solution)/shard_map/reduce_scatter | solution.py:295
  1275.0 19.8 %all-reduce.7 = (f32[4608]{0:T(1024)}, f32[768]{0:T(1024)}, f32[768]{0:T(1024)}, f32[3072]{0:T(1024)}, f32[768]{0:T(1024)}) all-reduce(f32[4608]{0:T(1024)} %get-tuple-element.259, f32[768]{0:T(1024)} %get-tuple-element.162, f32[768]{0:T(1024)} %get-tuple-element.159, ...), channel_id=3, replica_groups=mesh['dp'=8,'sp'=4] {'sp'}, use_global_device_ids=true, to_apply=%region_27.28.clone | all-reduce | flops 9984 | bytes 79872
  1301.5 24.7 %all-reduce.5 = (f32[1152]{0:T(1024)}, f32[192]{0:T(256)}, f32[192]{0:T(256)}, f32[768]{0:T(1024)}, f32[192]{0:T(256)}) all-reduce(f32[1152]{0:T(1024)} %dynamic-slice.1, f32[192]{0:T(256)} %dynamic-slice.3, f32[192]{0:T(256)} %dynamic-slice.5, f32[768]{0:T(1024)} %dynamic-slice.7, ...), channel_id=1, replica_groups=mesh['dp'=8,'sp'=4] {'dp'}, use_global_device_ids=true, to_apply=%region_28.29 | all-reduce | flops 2496 | bytes 19968 | tf_op jit(solution)/shard_map/psum | solution.py:303
  1326.2 17.2 %psum.77 = bf16[4,4608]{1,0:T(4,128)(2,1)} all-reduce(bf16[4,4608]{1,0:T(4,128)(2,1)} %get-tuple-element.260), channel_id=1, replica_groups=mesh['dp'=8,'sp'=4] {'sp'}, use_global_device_ids=true, to_apply=%region_23.24 | all-reduce | flops 18432 | bytes 73728 | tf_op jit(solution)/shard_map/psum | solution.py:287
  1352.3 62.5 %all-reduce.10.cloned.1.call-done = (f32[32,4608]{0,1:T(8,128)}, f32[192,2304]{1,0:T(8,128)}, f32[192,768]{1,0:T(8,128)}, f32[192,3072]{1,0:T(8,128)}, f32[768,768]{1,0:T(8,128)}) async-done(((f32[32,4608]{0,1:T(8,128)}, f32[192,2304]{1,0:T(8,128)}, f32[192,768]{1,0:T(8,128)}, f32[192,3072]{1,0:T(8,128)}, f32[768,768]{1,0:T(8,128)}), (f32[32,4608]{0,1:T(8,128)}, f32[192,2304]{1,0:T(8,128)}, ...) | async-done | bytes 7667728 | tf_op jit(solution)/shard_map/psum | solution.py:303
  (361 shorter events, 377.5 us)
Async XLA Ops:
  34.5 111.3 %all-to-all-start = ((bf16[4,256,3,768]{1,0,2,3:T(4,128)(2,1)}), bf16[4,256,3,768]{1,0,2,3:T(4,128)(2,1)}, u32[]{:S(2)}, u32[]{:S(2)}) async-start(bf16[4,256,3,768]{1,0,2,3:T(4,128)(2,1)} %copy.117), calls=%async_computation | async-start | bytes 9437184 | tf_op jit(solution)/shard_map/all_to_all | solution.py:175
  257.6 56.4 %copy-start.33 = (f32[4,768]{1,0:T(4,128)S(1)}, f32[4,768]{1,0:T(4,128)}, u32[]{:S(2)}) copy-start(f32[4,768]{1,0:T(4,128)} %get-tuple-element.266) | copy-start | bytes 36868
  257.6 52.3 %all-to-all-start.1 = ((bf16[4,1024,192]{2,0,1:T(4,128)(2,1)}), bf16[4,1024,192]{2,0,1:T(4,128)(2,1)}, u32[]{:S(2)}, u32[]{:S(2)}) async-start(bf16[4,1024,192]{2,0,1:T(4,128)(2,1)} %copy.120), calls=%async_computation.1 | async-start | bytes 4194304 | tf_op jit(solution)/shard_map/all_to_all | solution.py:177
  262.2 503.5 %reduce-scatter.16.cloned.1.call-start = ((), (), s32[]{:S(2)}) async-start(), calls=%async_computation.13 | async-start | bytes 2949120
  263.2 92.7 %copy-start.26 = (f32[768]{0:T(1024)}, f32[768]{0:T(1024)S(1)}, u32[]{:S(2)}) copy-start(f32[768]{0:T(1024)S(1)} %convert_element_type.129) | copy-start | bytes 9220
  318.1 37.7 %copy-start.8 = (f32[4,256,768]{2,1,0:T(8,128)}, f32[4,256,768]{2,1,0:T(8,128)S(1)}, u32[]{:S(2)}) copy-start(f32[4,256,768]{2,1,0:T(8,128)S(1)} %get-tuple-element.217) | copy-start | bytes 9437188
  318.2 37.7 %copy-start.28 = (f32[4,256]{1,0:T(4,128)}, f32[4,256]{1,0:T(4,128)S(1)}, u32[]{:S(2)}) copy-start(f32[4,256]{1,0:T(4,128)S(1)} %broadcast_multiply_fusion.6) | copy-start | bytes 12292
  318.7 37.2 %copy-start.29 = (f32[4,256]{1,0:T(4,128)}, f32[4,256]{1,0:T(4,128)S(1)}, u32[]{:S(2)}) copy-start(f32[4,256]{1,0:T(4,128)S(1)} %add_rsqrt_fusion) | copy-start | bytes 12292
  342.8 13.0 copy-start.14
  342.8 13.0 copy-start.50
  355.9 17.1 %copy-start.20 = (bf16[768,768]{1,0:T(8,128)(2,1)S(1)}, bf16[768,768]{1,0:T(8,128)(2,1)}, u32[]{:S(2)}) copy-start(bf16[768,768]{1,0:T(8,128)(2,1)} %param.23) | copy-start | bytes 3538948
  439.3 8.3 copy-start.12
  439.3 8.4 copy-start.13
  481.5 8.3 copy-start.12
  481.5 8.4 copy-start.13
  523.6 8.3 copy-start.12
  523.6 8.4 copy-start.13
  565.8 8.3 copy-start.12
  565.8 8.4 copy-start.13
  718.5 97.0 %reduce-scatter.10.cloned.1.call-start = ((), (), s32[]{:S(2)}) async-start(), calls=%async_computation.10 | async-start | bytes 2949120 | tf_op jit(solution)/shard_map/reduce_scatter | solution.py:296
  723.7 255.0 %reduce-scatter.12.cloned.1.call-start = ((), (), s32[]{:S(2)}) async-start(), calls=%async_computation.11 | async-start | bytes 11796480 | tf_op jit(solution)/shard_map/reduce_scatter | solution.py:298
  734.7 408.4 %reduce-scatter.14.cloned.1.call-start = ((), (), s32[]{:S(2)}) async-start(), calls=%async_computation.12 | async-start | bytes 11796480 | tf_op jit(solution)/shard_map/reduce_scatter | solution.py:300
  749.1 520.5 %reduce-scatter.8.cloned.1.call-start = ((), (), s32[]{:S(2)}) async-start(), calls=%async_computation.9 | async-start | bytes 8847360 | tf_op jit(solution)/shard_map/reduce_scatter | solution.py:295
  760.0 654.8 %all-reduce.10.cloned.1.call-start = ((), (), s32[]{:S(2)}) async-start(), calls=%async_computation.14 | async-start | bytes 18874368 | tf_op jit(solution)/shard_map/psum | solution.py:303
  (70 other events, 258.6 us)
Sparse Core Ops, SparseCore 0:
  718.6 46.9 reduce-scatter.15
  768.0 47.5 reduce-scatter.9
  817.9 160.7 reduce-scatter.11
  980.9 162.1 reduce-scatter.13
  1145.2 124.2 reduce-scatter.7
  1274.3 140.4 all-reduce.9
